TPU v7x, 256 devices: a whole 4x4x8 slice. The times are simulated.
256 devices in a mesh: group: 8 (over x, core), expert: 32 (over y, z).
Axes of the slice: x: 4, y: 4, z: 8, core: 2. Of those that a mesh axis runs over, the one named last changes fastest.
Arguments:
- resid: bfloat16 [32768, 2048], P(('group', 'expert')), may hold values from -6 to 6
- queries: bfloat16 [32768, 2048], P(('group', 'expert')), may hold values from -48 to 48
- span_kv: bfloat16 [2, 32768, 2048], P(None, ('group', 'expert')), may hold values from -4 to 4
- cache_kv: bfloat16 [2, 256, 2, 128, 2048], P(None, ('group', 'expert')), may hold values from -6 to 6
- seg_len: int32 [256, 2], P(('group', 'expert')), may hold values from 0 to 128, as said below
- o_rows: bfloat16 [2048, 2048], P('expert'), may hold values from -0.125 to 0.125
- norm_gain: float32 [2048], replicated, may hold values from 0.25 to 1.75
- routes: int32 [32768, 8], P(('group', 'expert')), may hold values from 0 to 31, all different within a row; in each aligned block of 128 rows (0 to 127, 128 to 255, ...) at most 48 rows name the same one
- route_wts: float32 [32768, 8], P(('group', 'expert')), may hold values from 0.05 to 0.6
- w_in: bfloat16 [32, 2048, 1024], P('expert'), may hold values from -0.125 to 0.125
- w_out: bfloat16 [32, 512, 2048], P('expert'), may hold values from -0.25 to 0.25
Outputs:
- layer_out: bfloat16 [32768, 2048], P(('group', 'expert'))
Inputs may be any that keep to these rules, and one draw needn't show every extreme that they name: seg_len[d, 0] is 1 to 128; seg_len[d, 1] is 0 (the paired request is short) or 1 to 128; seg_len[0, 0] and seg_len[0, 1] are 128 and seg_len[1, 1] is 0. `routes`: each row names 8 different experts; among the 128 rows of one device no expert is named more than 48 times.
All inputs are finite; a program needn't handle non-finite values.
Results may differ from a plain program's by a relative error of at most 0.0053.
Values may be sent and summed in bfloat16 or wider, within the bound.
A program may use at most 128 MiB of HBM per device.

v0:
```python
import math
import jax
import jax.numpy as jnp
from jax import lax
from jax.sharding import PartitionSpec as P

HEADS = 16
HD = 128
FF = 512
TOPK = 8


def swapped(block, axis, distance):
    count = lax.axis_size(axis)
    route = []
    for low in range(count):
        high = low | 1 << distance
        if high != low and high < count:
            route += [(low, high), (high, low)]
    return lax.ppermute(block, axis, route)


def attend(query_rows, key_rows, value_rows, valid_keys):
    q_heads = query_rows.reshape(query_rows.shape[0], HEADS, HD)
    k_heads = key_rows.reshape(key_rows.shape[0], HEADS, HD)
    v_heads = value_rows.reshape(value_rows.shape[0], HEADS, HD)
    scores = jnp.einsum("chd,shd->hcs", q_heads, k_heads, preferred_element_type=jnp.float32) * (
        1.0 / math.sqrt(HD)
    )
    scores = jnp.where(valid_keys[None, None, :], scores, -1e30)
    peak_score = jnp.max(scores, axis=-1)
    expo = jnp.where(valid_keys[None, None, :], jnp.exp(scores - peak_score[..., None]), 0.0)
    totals = jnp.sum(expo, axis=-1)
    probs_low = expo.astype(jnp.bfloat16)
    accum_out = jnp.einsum("hcs,shd->chd", probs_low, v_heads, preferred_element_type=jnp.float32)
    return (peak_score, totals, accum_out)


def merge_parts(first, second):
    peak_a, total_a, accum_a = first
    peak_b, total_b, accum_b = second
    peak_both = jnp.maximum(peak_a, peak_b)
    scale_a = jnp.exp(peak_a - peak_both).T
    scale_b = jnp.exp(peak_b - peak_both).T
    numer = accum_a * scale_a[:, :, None] + accum_b * scale_b[:, :, None]
    denom = total_a.T * scale_a + total_b.T * scale_b
    merged = numer / denom[:, :, None]
    return merged.reshape(merged.shape[0], -1).astype(jnp.bfloat16)


def expert_mlp(token_rows, weight_in, weight_out):
    joined = jnp.dot(token_rows, weight_in, preferred_element_type=jnp.float32)
    hidden = (jax.nn.silu(joined[:, :FF]) * joined[:, FF:]).astype(jnp.bfloat16)
    return jnp.dot(hidden, weight_out, preferred_element_type=jnp.float32).astype(jnp.bfloat16)


def shards(
    resid, queries, span_kv, cache_kv, seg_len, o_rows, norm_gain, routes, route_wts, w_in, w_out
):
    span_rows = queries.shape[0]
    seg_rows = cache_kv.shape[3]
    width = queries.shape[1]
    experts_here = lax.axis_size("expert")
    positions = jnp.arange(seg_rows, dtype=jnp.int32)
    keys_a = jnp.concatenate([span_kv[0], cache_kv[0, 0, 0]], axis=0)
    vals_a = jnp.concatenate([span_kv[1], cache_kv[1, 0, 0]], axis=0)
    valid_a = jnp.concatenate([jnp.ones((span_rows,), bool), positions < seg_len[0, 0]])
    part_a = attend(queries, keys_a, vals_a, valid_a)
    length_low = seg_len[0, 1:2].astype(jnp.float32).astype(jnp.bfloat16)
    fetched, fetched_len = swapped((cache_kv[:, 0, 1], length_low), "group", 0)
    valid_b = positions.astype(jnp.float32) < fetched_len[0].astype(jnp.float32)
    part_b = attend(queries, fetched[0], fetched[1], valid_b)
    attended = merge_parts(part_a, part_b)
    projected = jnp.dot(
        attended,
        lax.all_gather(o_rows, "expert", axis=0, tiled=True),
        preferred_element_type=jnp.float32,
    )
    residual = resid.astype(jnp.float32) + projected
    normed = (
        residual
        * lax.rsqrt(jnp.mean(residual * residual, axis=-1, keepdims=True) + 1e-05)
        * norm_gain
    ).astype(jnp.bfloat16)
    capacity = min(span_rows, span_rows * TOPK * 3 // (2 * experts_here))
    onehot = (
        routes[:, :, None] == jnp.arange(experts_here, dtype=jnp.int32)[None, None, :]
    ).astype(jnp.int32)
    counts = jnp.sum(onehot, axis=1)
    before = jnp.cumsum(counts, axis=0) - counts
    slot_ids = jnp.sum(onehot * before[:, None, :], axis=-1)
    flat_slot = routes * capacity + slot_ids
    placing = jnp.any(
        flat_slot[None, :, :]
        == jnp.arange(experts_here * capacity, dtype=jnp.int32)[:, None, None],
        axis=-1,
    )
    outgoing = jnp.dot(
        placing.astype(jnp.bfloat16), normed, preferred_element_type=jnp.float32
    ).astype(jnp.bfloat16)
    outgoing = outgoing.reshape(experts_here, capacity, width)
    arrived = lax.all_to_all(outgoing, "expert", split_axis=0, concat_axis=0, tiled=True)
    flat_rows = arrived.reshape(-1, width)
    output_rows = expert_mlp(flat_rows, w_in[0], w_out[0]).reshape(arrived.shape)
    returned_rows = lax.all_to_all(output_rows, "expert", split_axis=0, concat_axis=0, tiled=True)
    returned_rows = returned_rows.reshape(experts_here * capacity, width)
    expert_sum = jnp.zeros((span_rows, width), jnp.float32)
    for route_k in range(TOPK):
        picked = returned_rows[flat_slot[:, route_k]].astype(jnp.float32)
        expert_sum = expert_sum + route_wts[:, route_k, None] * picked
    return (residual + expert_sum).astype(jnp.bfloat16)


def solution(mesh):
    placed = (
        P(("group", "expert"), None),
        P(("group", "expert"), None),
        P(None, ("group", "expert"), None),
        P(None, ("group", "expert"), None, None, None),
        P(("group", "expert"), None),
        P("expert", None),
        P(),
        P(("group", "expert"), None),
        P(("group", "expert"), None),
        P("expert", None, None),
        P("expert", None, None),
    )
    return jax.shard_map(
        shards, mesh=mesh, in_specs=placed, out_specs=P(("group", "expert"), None), check_vma=False
    )
```

profile of v0, /device:TPU:33, one launch (start us, length us, event | category | flops | bytes accessed | tf_op | source)
XLA Modules:
  0.0 479.4 jit_solution(5816244615594503621)
XLA Ops:
  9.2 1.6 collective-permute-start
  13.4 2.1 fusion.65
  17.9 2.3 fusion.63
  23.6 2.1 copy.36
  26.8 5.6 %fusion = pred[1536,128]{1,0:T(8,128)(4,1)S(1)} fusion(s32[128,8]{0,1:T(8,128)S(1)} %multiply_add_fusion), kind=kLoop, calls=%fused_computation.11 | loop fusion | flops 2949120 | bytes 200704 | tf_op jit(solution)/shard_map/reduce_or | solution.py:93
  32.4 1.9 bitcast_reduce_fusion
  37.0 1.4 fusion.64
  41.2 67.1 %all-gather.2.cloned.1.call-done = bf16[2048,2048]{1,0:T(8,128)(2,1)} async-done(((bf16[64,2048]{1,0:T(8,128)(2,1)}), bf16[2048,2048]{1,0:T(8,128)(2,1)}) %all-gather.2.cloned.1.call-update) | async-done | bytes 8388624 | tf_op jit(solution)/shard_map/all_gather | solution.py:76
  108.3 4.9 %multiply_reduce_fusion = (f32[128]{0:T(128)S(1)}, f32[128,2048]{1,0:T(8,128)S(1)}) fusion(bf16[128,2048]{0,1:T(8,128)(2,1)} %bitcast.126, bf16[2048,2048]{1,0:T(8,128)(2,1)} %all-gather.2.cloned.1.call-done, bf16[128,2048]{1,0:T(8,128)(2,1)} %param.11), kind=kOutput, calls=%fused_computation.44 | convolution fusion | flops 1074790272 | bytes 10486272 | tf_op jit(solution)/shard_map/dot_general | solution.py:74
  113.2 1.9 convolution_convert_fusion.1
  115.1 145.8 %all_to_all.10 = bf16[32,48,2048]{2,1,0:T(8,128)(2,1)S(1)} all-to-all(bf16[32,48,2048]{2,1,0:T(8,128)(2,1)S(1)} %bitcast.120), channel_id=1, replica_groups=mesh['group'=8,'expert'=32] {'expert'}, dimensions={0} | all-to-all | bytes 12582912 | tf_op jit(solution)/shard_map/all_to_all | solution.py:102
  260.9 6.8 %fusion.1 = f32[1536,1024]{1,0:T(8,128)S(1)} fusion(bf16[1536,2048]{1,0:T(8,128)(2,1)S(1)} %bitcast.122, bf16[1,2048,1024]{2,1,0:T(8,128)(2,1)S(1)} %copy-done.9), kind=kOutput, calls=%fused_computation.12 | convolution fusion | flops 6442450944 | bytes 16777216 | tf_op jit(solution)/shard_map/dot_general | solution.py:52
  267.7 5.4 %convolution_convert_fusion = bf16[1536,2048]{1,0:T(8,128)(2,1)} fusion(bf16[1,512,2048]{2,1,0:T(8,128)(2,1)S(1)} %copy-done, f32[1536,1024]{1,0:T(8,128)S(1)} %fusion.1), kind=kOutput, calls=%fused_computation.8 | convolution fusion | flops 3229089792 | bytes 14680064 | tf_op jit(solution)/shard_map/dot_general | solution.py:54
  273.1 7.4 %all-to-all-start.1 = ((bf16[32,48,2048]{2,1,0:T(8,128)(2,1)}), bf16[32,48,2048]{2,1,0:T(8,128)(2,1)}, u32[]{:S(2)}, u32[]{:S(2)}) async-start(bf16[32,48,2048]{2,1,0:T(8,128)(2,1)} %bitcast.121), calls=%async_computation.1 | async-start | bytes 12582912 | tf_op jit(solution)/shard_map/all_to_all | solution.py:105
  280.6 140.9 %all-to-all-done.1 = bf16[32,48,2048]{2,1,0:T(8,128)(2,1)} async-done(((bf16[32,48,2048]{2,1,0:T(8,128)(2,1)}), bf16[32,48,2048]{2,1,0:T(8,128)(2,1)}, u32[]{:S(2)}, u32[]{:S(2)}) %all-to-all-start.1) | async-done | bytes 6291488 | tf_op jit(solution)/shard_map/all_to_all | solution.py:105
  421.5 5.8 %gather_fusion = bf16[128,2048]{1,0:T(8,128)(2,1)} fusion(bf16[1536,2048]{1,0:T(8,128)(2,1)} %bitcast.24, s32[1024]{0:T(1024)S(1)} %get-tuple-element.45), kind=kCustom, calls=%fused_computation | custom fusion | bytes 1049088 | tf_op jit(solution)/shard_map/gather | solution.py:109
  427.3 5.9 %gather_fusion.1 = bf16[128,2048]{1,0:T(8,128)(2,1)} fusion(bf16[1536,2048]{1,0:T(8,128)(2,1)} %bitcast.24, s32[1024]{0:T(1024)S(1)} %get-tuple-element.44), kind=kCustom, calls=%fused_computation.1 | custom fusion | bytes 1049088 | tf_op jit(solution)/shard_map/gather | solution.py:109
  433.2 5.9 %gather_fusion.2 = bf16[128,2048]{1,0:T(8,128)(2,1)} fusion(bf16[1536,2048]{1,0:T(8,128)(2,1)} %bitcast.24, s32[1024]{0:T(1024)S(1)} %get-tuple-element.43), kind=kCustom, calls=%fused_computation.2 | custom fusion | bytes 1049088 | tf_op jit(solution)/shard_map/gather | solution.py:109
  439.1 5.9 %gather_fusion.3 = bf16[128,2048]{1,0:T(8,128)(2,1)} fusion(bf16[1536,2048]{1,0:T(8,128)(2,1)} %bitcast.24, s32[1024]{0:T(1024)S(1)} %get-tuple-element.42), kind=kCustom, calls=%fused_computation.3 | custom fusion | bytes 1049088 | tf_op jit(solution)/shard_map/gather | solution.py:109
  444.9 5.8 %gather_fusion.4 = bf16[128,2048]{1,0:T(8,128)(2,1)} fusion(bf16[1536,2048]{1,0:T(8,128)(2,1)} %bitcast.24, s32[1024]{0:T(1024)S(1)} %get-tuple-element.41), kind=kCustom, calls=%fused_computation.4 | custom fusion | bytes 1049088 | tf_op jit(solution)/shard_map/gather | solution.py:109
  450.7 5.8 %gather_fusion.5 = bf16[128,2048]{1,0:T(8,128)(2,1)} fusion(bf16[1536,2048]{1,0:T(8,128)(2,1)} %bitcast.24, s32[1024]{0:T(1024)S(1)} %get-tuple-element.40), kind=kCustom, calls=%fused_computation.5 | custom fusion | bytes 1049088 | tf_op jit(solution)/shard_map/gather | solution.py:109
  456.6 6.1 %gather_fusion.6 = bf16[128,2048]{1,0:T(8,128)(2,1)} fusion(bf16[1536,2048]{1,0:T(8,128)(2,1)} %bitcast.24, s32[1024]{0:T(1024)S(1)} %get-tuple-element.39), kind=kCustom, calls=%fused_computation.6 | custom fusion | bytes 1049088 | tf_op jit(solution)/shard_map/gather | solution.py:109
  462.6 5.8 %gather_fusion.7 = bf16[128,2048]{1,0:T(8,128)(2,1)} fusion(bf16[1536,2048]{1,0:T(8,128)(2,1)} %bitcast.24, s32[1024]{0:T(1024)S(1)} %get-tuple-element.38), kind=kCustom, calls=%fused_computation.7 | custom fusion | bytes 1049088 | tf_op jit(solution)/shard_map/gather | solution.py:109
  468.5 3.9 add_convert_fusion
  (56 shorter events, 16.3 us)
Async XLA Ops:
  6.5 261.2 %copy-start = (bf16[1,512,2048]{2,1,0:T(8,128)(2,1)S(1)}, bf16[1,512,2048]{2,1,0:T(8,128)(2,1)}, u32[]{:S(2)}) copy-start(bf16[1,512,2048]{2,1,0:T(8,128)(2,1)} %param.21) | copy-start | bytes 6291460
  6.5 101.7 %all-gather.2.cloned.1.call-start = ((), (), s32[]{:S(2)}) async-start(), calls=%async_computation.2 | async-start | bytes 8650752 | tf_op jit(solution)/shard_map/all_gather | solution.py:76
  9.2 27.0 %collective-permute-start = (bf16[1]{0:T(256)(128)(2,1)}, bf16[1]{0:T(256)(128)(2,1)}, u32[]{:S(2)}, u32[]{:S(2)}) collective-permute-start(bf16[1]{0:T(256)(128)(2,1)} %bitcast.8), channel_id=1, source_target_pairs={{0,32},{32,0},{64,96},{96,64},{128,160},{160,128},{192,224},{224,1... | collective-permute-start | bytes 14 | tf_op jit(solution)/shard_map/ppermute | solution.py:20
  13.4 23.5 %collective-permute-start.1 = (bf16[2,128,2048]{1,2,0:T(8,128)(2,1)}, bf16[2,128,2048]{1,2,0:T(8,128)(2,1)}, u32[]{:S(2)}, u32[]{:S(2)}) collective-permute-start(bf16[2,128,2048]{1,2,0:T(8,128)(2,1)} %bitcast.127), channel_id=1, source_target_pairs={{0,32},{32,0},{64,96},{96,64},{128,160},{160,128},{192,224},{224,1... | collective-permute-start | bytes 3145736 | tf_op jit(solution)/shard_map/ppermute | solution.py:20
  17.9 7.8 %copy-start.6 = (s32[128,8]{0,1:T(8,128)S(1)}, s32[128,8]{0,1:T(8,128)}, u32[]{:S(2)}) copy-start(s32[128,8]{0,1:T(8,128)} %param.18) | copy-start | bytes 12292
  34.2 1.4 copy-start.1
  34.2 4.2 copy-start.3
  36.2 3.0 copy-start.4
  36.9 2.3 copy-start.2
  36.9 2.3 copy-start.5
  108.3 5.0 %copy-start.7 = (f32[2048]{0:T(1024)S(1)}, f32[2048]{0:T(1024)}, u32[]{:S(2)}) copy-start(f32[2048]{0:T(1024)} %param.17) | copy-start | bytes 24580
  115.1 145.8 %copy-start.9 = (bf16[1,2048,1024]{2,1,0:T(8,128)(2,1)S(1)}, bf16[1,2048,1024]{2,1,0:T(8,128)(2,1)}, u32[]{:S(2)}) copy-start(bf16[1,2048,1024]{2,1,0:T(8,128)(2,1)} %param.20) | copy-start | bytes 12582916
  273.1 7.4 %copy-start.8 = (f32[128,8]{0,1:T(8,128)S(1)}, f32[128,8]{0,1:T(8,128)}, u32[]{:S(2)}) copy-start(f32[128,8]{0,1:T(8,128)} %param.19) | copy-start | bytes 12292
  273.1 148.4 %all-to-all-start.1 = ((bf16[32,48,2048]{2,1,0:T(8,128)(2,1)}), bf16[32,48,2048]{2,1,0:T(8,128)(2,1)}, u32[]{:S(2)}, u32[]{:S(2)}) async-start(bf16[32,48,2048]{2,1,0:T(8,128)(2,1)} %bitcast.121), calls=%async_computation.1 | async-start | bytes 12582912 | tf_op jit(solution)/shard_map/all_to_all | solution.py:105
Sparse Core Ops, SparseCore 0:
  9.9 98.2 all-gather.1
where the time goes:
time: 489 us; the launch traced here: 479 us
  waiting for transfers between devices  209 us (43%)
  blocking collectives  146 us (30%)
  local copies, waits for them, and re-layouts  66.1 us (14%)
  matrix products  23.3 us (5%)
  between operations  15.3 us (3%)
  other arithmetic  11.2 us (2%)
  starting transfers between devices  8.94 us (2%)
    all_to_all x1, blocking collectives, shards(): lax.all_to_all(outgoing, 'expert', split_axis=0, concat_axis=0, tiled=True)  146 us
    all_to_all x1, waiting for transfers between devices, shards(): lax.all_to_all(output_rows, 'expert', split_axis=0, concat_axis=0, tiled=...  141 us
    all_gather x1, waiting for transfers between devices, shards(): lax.all_gather(o_rows, 'expert', axis=0, tiled=True)  67.1 us
    gather x8, local copies, waits for them, and re-layouts, shards(): picked = returned_rows[flat_slot[:, route_k]].astype(jnp.float32)  47 us
  transfers between devices with their start and end apart: 4, of which 2 were waited for; matrix products, arithmetic and copies ran while one was open for 6% of the time, Pallas kernels for 0%

commit v1 on v0

--- a/solution.py
+++ b/solution.py
@@ -73,7 +73,9 @@
     attended = merge_parts(part_a, part_b)
     projected = jnp.dot(
         attended,
-        lax.all_gather(o_rows, "expert", axis=0, tiled=True),
+        jnp.concatenate(
+            lax.all_to_all(jnp.stack([o_rows] * lax.axis_size("expert")), "expert", 0, 0), axis=0
+        ),
         preferred_element_type=jnp.float32,
     )
     residual = resid.astype(jnp.float32) + projected

time: 489 us -> 576 us (1.18); the launches traced: 479 us -> 573 us
  waiting for transfers between devices: 209 us -> 298 us
  between operations: 15.3 us -> 1.98 us
  starting transfers between devices: 8.94 us -> 20.1 us
    all_to_all x0 -> x1, waiting for transfers between devices: none -> 158 us  [shards(): lax.all_to_all(jnp.stack([o_rows] * lax.axis_size('expert')), 'expert', 0...]
    all_gather x1 -> x0, waiting for transfers between devices: 67.1 us -> none  [shards(): lax.all_gather(o_rows, 'expert', axis=0, tiled=True)]
    all_to_all x0 -> x1, starting transfers between devices: none -> 11 us  [shards(): lax.all_to_all(jnp.stack([o_rows] * lax.axis_size('expert')), 'expert', 0...]
  transfers between devices with their start and end apart: 4 -> 4, of which waited for: 2 -> 2; matrix products, arithmetic and copies ran while one was open for 6% -> 5% of each run, Pallas kernels for 0% -> 0%
where the time goes in v1:
time: 576 us; the launch traced here: 573 us
  waiting for transfers between devices  298 us (52%)
  blocking collectives  148 us (26%)
  local copies, waits for them, and re-layouts  69.3 us (12%)
  matrix products  23.4 us (4%)
  starting transfers between devices  20.1 us (3%)
  other arithmetic  11.2 us (2%)
    all_to_all x1, waiting for transfers between devices, shards(): lax.all_to_all(jnp.stack([o_rows] * lax.axis_size('expert')), 'expert', 0...  158 us
    all_to_all x1, blocking collectives, shards(): lax.all_to_all(outgoing, 'expert', split_axis=0, concat_axis=0, tiled=True)  148 us
    all_to_all x1, waiting for transfers between devices, shards(): lax.all_to_all(output_rows, 'expert', split_axis=0, concat_axis=0, tiled=...  141 us
    gather x8, local copies, waits for them, and re-layouts, shards(): picked = returned_rows[flat_slot[:, route_k]].astype(jnp.float32)  47 us
  transfers between devices with their start and end apart: 4, of which 2 were waited for; matrix products, arithmetic and copies ran while one was open for 5% of the time, Pallas kernels for 0%

profile of v1, /device:TPU:33, one launch (start us, length us, event | category | flops | bytes accessed | tf_op | source)
XLA Modules:
  0.0 572.7 jit_solution(9070720545504948641)
XLA Ops:
  0.0 5.4 stack.2
  5.4 11.0 %all-to-all-start = ((bf16[32,64,2048]{2,1,0:T(8,128)(2,1)}), bf16[32,64,2048]{2,1,0:T(8,128)(2,1)}, u32[]{:S(2)}, u32[]{:S(2)}) async-start(bf16[32,64,2048]{2,1,0:T(8,128)(2,1)} %stack.2), calls=%async_computation | async-start | bytes 16777216 | tf_op jit(solution)/shard_map/all_to_all | solution.py:77
  17.6 2.1 collective-permute-start
  21.4 2.1 fusion.65
  25.8 2.3 fusion.63
  31.4 2.0 copy.36
  34.6 5.6 fusion
  49.0 157.6 %all-to-all-done = bf16[32,64,2048]{2,1,0:T(8,128)(2,1)} async-done(((bf16[32,64,2048]{2,1,0:T(8,128)(2,1)}), bf16[32,64,2048]{2,1,0:T(8,128)(2,1)}, u32[]{:S(2)}, u32[]{:S(2)}) %all-to-all-start) | async-done | bytes 8388640 | tf_op jit(solution)/shard_map/all_to_all | solution.py:77
  206.6 4.9 multiply_reduce_fusion
  211.6 1.9 convolution_convert_fusion.1
  213.4 148.4 %all_to_all.15 = bf16[32,48,2048]{2,1,0:T(8,128)(2,1)S(1)} all-to-all(bf16[32,48,2048]{2,1,0:T(8,128)(2,1)S(1)} %bitcast.121), channel_id=1, replica_groups=mesh['group'=8,'expert'=32] {'expert'}, dimensions={0} | all-to-all | bytes 12582912 | tf_op jit(solution)/shard_map/all_to_all | solution.py:104
  361.9 6.8 %fusion.1 = f32[1536,1024]{1,0:T(8,128)S(1)} fusion(bf16[1536,2048]{1,0:T(8,128)(2,1)S(1)} %bitcast.123, bf16[1,2048,1024]{2,1,0:T(8,128)(2,1)S(1)} %copy-done.10), kind=kOutput, calls=%fused_computation.12 | convolution fusion | flops 6442450944 | bytes 16777216 | tf_op jit(solution)/shard_map/dot_general | solution.py:52
  368.7 5.4 convolution_convert_fusion
  374.1 6.7 %all-to-all-start.2 = ((bf16[32,48,2048]{2,1,0:T(8,128)(2,1)}), bf16[32,48,2048]{2,1,0:T(8,128)(2,1)}, u32[]{:S(2)}, u32[]{:S(2)}) async-start(bf16[32,48,2048]{2,1,0:T(8,128)(2,1)} %bitcast.122), calls=%async_computation.2 | async-start | bytes 12582912 | tf_op jit(solution)/shard_map/all_to_all | solution.py:107
  380.9 140.7 %all-to-all-done.2 = bf16[32,48,2048]{2,1,0:T(8,128)(2,1)} async-done(((bf16[32,48,2048]{2,1,0:T(8,128)(2,1)}), bf16[32,48,2048]{2,1,0:T(8,128)(2,1)}, u32[]{:S(2)}, u32[]{:S(2)}) %all-to-all-start.2) | async-done | bytes 6291488 | tf_op jit(solution)/shard_map/all_to_all | solution.py:107
  521.6 5.8 %gather_fusion = bf16[128,2048]{1,0:T(8,128)(2,1)} fusion(bf16[1536,2048]{1,0:T(8,128)(2,1)} %bitcast.25, s32[1024]{0:T(1024)S(1)} %get-tuple-element.45), kind=kCustom, calls=%fused_computation | custom fusion | bytes 1049088 | tf_op jit(solution)/shard_map/gather | solution.py:111
  527.4 5.9 %gather_fusion.1 = bf16[128,2048]{1,0:T(8,128)(2,1)} fusion(bf16[1536,2048]{1,0:T(8,128)(2,1)} %bitcast.25, s32[1024]{0:T(1024)S(1)} %get-tuple-element.44), kind=kCustom, calls=%fused_computation.1 | custom fusion | bytes 1049088 | tf_op jit(solution)/shard_map/gather | solution.py:111
  533.3 5.9 %gather_fusion.2 = bf16[128,2048]{1,0:T(8,128)(2,1)} fusion(bf16[1536,2048]{1,0:T(8,128)(2,1)} %bitcast.25, s32[1024]{0:T(1024)S(1)} %get-tuple-element.43), kind=kCustom, calls=%fused_computation.2 | custom fusion | bytes 1049088 | tf_op jit(solution)/shard_map/gather | solution.py:111
  539.2 5.9 %gather_fusion.3 = bf16[128,2048]{1,0:T(8,128)(2,1)} fusion(bf16[1536,2048]{1,0:T(8,128)(2,1)} %bitcast.25, s32[1024]{0:T(1024)S(1)} %get-tuple-element.42), kind=kCustom, calls=%fused_computation.3 | custom fusion | bytes 1049088 | tf_op jit(solution)/shard_map/gather | solution.py:111
  545.0 5.8 %gather_fusion.4 = bf16[128,2048]{1,0:T(8,128)(2,1)} fusion(bf16[1536,2048]{1,0:T(8,128)(2,1)} %bitcast.25, s32[1024]{0:T(1024)S(1)} %get-tuple-element.41), kind=kCustom, calls=%fused_computation.4 | custom fusion | bytes 1049088 | tf_op jit(solution)/shard_map/gather | solution.py:111
  550.8 5.8 %gather_fusion.5 = bf16[128,2048]{1,0:T(8,128)(2,1)} fusion(bf16[1536,2048]{1,0:T(8,128)(2,1)} %bitcast.25, s32[1024]{0:T(1024)S(1)} %get-tuple-element.40), kind=kCustom, calls=%fused_computation.5 | custom fusion | bytes 1049088 | tf_op jit(solution)/shard_map/gather | solution.py:111
  556.7 6.1 %gather_fusion.6 = bf16[128,2048]{1,0:T(8,128)(2,1)} fusion(bf16[1536,2048]{1,0:T(8,128)(2,1)} %bitcast.25, s32[1024]{0:T(1024)S(1)} %get-tuple-element.39), kind=kCustom, calls=%fused_computation.6 | custom fusion | bytes 1049088 | tf_op jit(solution)/shard_map/gather | solution.py:111
  562.8 5.8 %gather_fusion.7 = bf16[128,2048]{1,0:T(8,128)(2,1)} fusion(bf16[1536,2048]{1,0:T(8,128)(2,1)} %bitcast.25, s32[1024]{0:T(1024)S(1)} %get-tuple-element.38), kind=kCustom, calls=%fused_computation.7 | custom fusion | bytes 1049088 | tf_op jit(solution)/shard_map/gather | solution.py:111
  568.6 3.9 add_convert_fusion
  (59 shorter events, 17.0 us)
Async XLA Ops:
  0.0 368.7 %copy-start = (bf16[1,512,2048]{2,1,0:T(8,128)(2,1)S(1)}, bf16[1,512,2048]{2,1,0:T(8,128)(2,1)}, u32[]{:S(2)}) copy-start(bf16[1,512,2048]{2,1,0:T(8,128)(2,1)} %param.21) | copy-start | bytes 6291460
  5.4 11.0 %copy-start.9 = (s32[1,2]{1,0:T(1,128)S(1)}, s32[1,2]{1,0:T(1,128)}, u32[]{:S(2)}) copy-start(s32[1,2]{1,0:T(1,128)} %param.15) | copy-start | bytes 28
  5.4 14.4 %slice-start = ((bf16[2,1,2,128,2048]{4,3,2,1,0:T(8,128)(2,1)}), bf16[2,1,1,128,2048]{4,3,2,1,0:T(8,128)(2,1)S(1)}, s32[]{:S(2)}) async-start(bf16[2,1,2,128,2048]{4,3,2,1,0:T(8,128)(2,1)} %param.14), calls=%async_computation.3 | async-start | bytes 2097152 | tf_op jit(solution)/shard_map/slice | solution.py:70
  5.4 201.2 %all-to-all-start = ((bf16[32,64,2048]{2,1,0:T(8,128)(2,1)}), bf16[32,64,2048]{2,1,0:T(8,128)(2,1)}, u32[]{:S(2)}, u32[]{:S(2)}) async-start(bf16[32,64,2048]{2,1,0:T(8,128)(2,1)} %stack.2), calls=%async_computation | async-start | bytes 16777216 | tf_op jit(solution)/shard_map/all_to_all | solution.py:77
  17.6 26.4 %collective-permute-start = (bf16[1]{0:T(256)(128)(2,1)}, bf16[1]{0:T(256)(128)(2,1)}, u32[]{:S(2)}, u32[]{:S(2)}) collective-permute-start(bf16[1]{0:T(256)(128)(2,1)} %bitcast.8), channel_id=1, source_target_pairs={{0,32},{32,0},{64,96},{96,64},{128,160},{160,128},{192,224},{224,1... | collective-permute-start | bytes 14 | tf_op jit(solution)/shard_map/ppermute | solution.py:20
  21.1 23.7 %collective-permute-start.1 = (bf16[2,128,2048]{1,2,0:T(8,128)(2,1)}, bf16[2,128,2048]{1,2,0:T(8,128)(2,1)}, u32[]{:S(2)}, u32[]{:S(2)}) collective-permute-start(bf16[2,128,2048]{1,2,0:T(8,128)(2,1)} %bitcast.128), channel_id=1, source_target_pairs={{0,32},{32,0},{64,96},{96,64},{128,160},{160,128},{192,224},{224,1... | collective-permute-start | bytes 3145736 | tf_op jit(solution)/shard_map/ppermute | solution.py:20
  25.8 7.7 %copy-start.6 = (s32[128,8]{0,1:T(8,128)S(1)}, s32[128,8]{0,1:T(8,128)}, u32[]{:S(2)}) copy-start(s32[128,8]{0,1:T(8,128)} %param.18) | copy-start | bytes 12292
  42.0 1.4 copy-start.1
  42.0 4.2 copy-start.3
  44.0 3.0 copy-start.4
  44.8 2.3 copy-start.2
  44.8 2.3 copy-start.5
  206.6 5.0 copy-start.7
  213.4 148.5 %copy-start.10 = (bf16[1,2048,1024]{2,1,0:T(8,128)(2,1)S(1)}, bf16[1,2048,1024]{2,1,0:T(8,128)(2,1)}, u32[]{:S(2)}) copy-start(bf16[1,2048,1024]{2,1,0:T(8,128)(2,1)} %param.20) | copy-start | bytes 12582916
  374.1 6.8 %copy-start.8 = (f32[128,8]{0,1:T(8,128)S(1)}, f32[128,8]{0,1:T(8,128)}, u32[]{:S(2)}) copy-start(f32[128,8]{0,1:T(8,128)} %param.19) | copy-start | bytes 12292
  374.1 147.5 %all-to-all-start.2 = ((bf16[32,48,2048]{2,1,0:T(8,128)(2,1)}), bf16[32,48,2048]{2,1,0:T(8,128)(2,1)}, u32[]{:S(2)}, u32[]{:S(2)}) async-start(bf16[32,48,2048]{2,1,0:T(8,128)(2,1)} %bitcast.122), calls=%async_computation.2 | async-start | bytes 12582912 | tf_op jit(solution)/shard_map/all_to_all | solution.py:107
